TPU v7x, 256 devices: a whole 4x4x8 slice. The times are simulated.
256 devices in a mesh: block: 8 (over z), tile: 32 (over x, y, core).
Axes of the slice: x: 4, y: 4, z: 8, core: 2. Of those that a mesh axis runs over, the one named last changes fastest.
Arguments:
- acts: bfloat16 [16, 32, 64, 384], P('block', 'tile'), may hold values from -6 to 6
- gamma: float32 [384], replicated, may hold values from 0.25 to 1.75
- beta: float32 [384], replicated, may hold values from -3 to 3
- weights: bfloat16 [384, 27, 192], P('tile'), may hold values from -0.0625 to 0.0625
- cotangent: bfloat16 [16, 64, 128, 192], P('block', 'tile'), may hold values from -6 to 6
Outputs:
- d_acts: bfloat16 [16, 32, 64, 384], P('block', 'tile')
- d_weights: float32 [384, 27, 192], P('tile')
All inputs are finite; a program needn't handle non-finite values.
Results may differ from a plain program's by a relative error of at most 0.0029.
Values may be sent and summed in bfloat16 or wider, within the bound.
A program may use at most 128 MiB of HBM per device.

v0:
```python
import jax
import jax.numpy as jnp
from jax import lax
from jax.sharding import PartitionSpec as P

GROUPS = 32
norm_eps = 1e-06


def from_behind(value, axis, steps):
    count = lax.axis_size(axis)
    first, last = (max(0, -steps), min(count, count - steps))
    return lax.ppermute(value, axis, [(source, source + steps) for source in range(first, last)])


def padded_2(value, sides, width):
    for axis, dim in sides:
        size, length = (lax.axis_size(axis), value.shape[dim])
        up = [(i, (i + 1) % size) for i in range(size - 1)]
        down = [(j, i) for i, j in up]
        last = lax.slice_in_dim(value, length - width, length, axis=dim)
        first = lax.slice_in_dim(value, 0, width, axis=dim)
        before = lax.ppermute(last, axis, up)
        after = lax.ppermute(first, axis, down)
        value = jnp.concatenate([before, value, after], axis=dim)
    return value


def group_totals(values, frames, per_group):
    return jnp.sum(values, axis=(1, 2)).reshape(frames, GROUPS, per_group).sum(-1)


def shards(acts, gamma, beta, weights, cotangent):
    frames, low_rows, low_cols, channels = acts.shape
    tiles = lax.axis_size("tile")
    per_group = channels // GROUPS
    group_size = low_rows * tiles * low_cols * per_group
    acts_wide = acts.astype(jnp.float32)
    stat_sum = group_totals(acts_wide, frames, per_group)
    stat_sq = group_totals(acts_wide * acts_wide, frames, per_group)
    stat_sum, stat_sq = lax.psum((stat_sum, stat_sq), "tile")
    group_mean = stat_sum / group_size
    inv_std = lax.rsqrt(stat_sq / group_size - group_mean * group_mean + norm_eps)
    mean_chan = jnp.repeat(group_mean, per_group, axis=1)[:, None, None, :]
    inv_chan = jnp.repeat(inv_std, per_group, axis=1)[:, None, None, :]
    normed = (acts_wide - mean_chan) * inv_chan
    shifted = normed * gamma + beta
    gate_value = jax.nn.sigmoid(shifted)
    hidden = (shifted * gate_value).astype(jnp.bfloat16)
    previous = from_behind(hidden, "block", 1)
    joined = jnp.concatenate([previous, hidden], 0)
    padded = padded_2(joined, (("tile", 1),), 1)
    upsampled = jnp.repeat(jnp.repeat(padded, 2, axis=1), 2, axis=2)[:, 1 : 2 * low_rows + 3]
    upsampled = jnp.pad(upsampled, ((0, 0), (0, 0), (1, 1), (0, 0)))
    following = from_behind(cotangent, "block", -1)
    grad_field = jnp.concatenate([cotangent, following], 0)
    grad_field = padded_2(grad_field, (("tile", 1),), 1)
    grad_field = jnp.pad(grad_field, ((0, 0), (0, 0), (1, 1), (0, 0)))
    up_rows = 2 * low_rows
    up_cols = 2 * low_cols
    num_cells = frames * up_rows * up_cols
    tap_list = [(tap // 9, tap // 3 % 3, tap % 3) for tap in range(27)]
    windows = [
        grad_field[
            2 - tap_t : 2 - tap_t + frames,
            2 - tap_h : 2 - tap_h + up_rows,
            2 - tap_w : 2 - tap_w + up_cols,
        ].reshape(num_cells, -1)
        for tap_t, tap_h, tap_w in tap_list
    ]
    columns = jnp.concatenate(windows, 1)
    piece_rows = lax.all_gather(weights, "tile", axis=0, tiled=True)
    flat_rows = piece_rows.reshape(piece_rows.shape[0], -1)
    back_grad = lax.dot_general(
        columns, flat_rows, (((1,), (1,)), ((), ())), preferred_element_type=jnp.float32
    )
    back_grad = back_grad.reshape(frames, low_rows, 2, low_cols, 2, piece_rows.shape[0])
    act_grad = back_grad.sum(axis=(2, 4))
    silu_slope = gate_value * (1.0 + shifted * (1.0 - gate_value))
    norm_grad = act_grad * silu_slope * gamma
    first_sum = group_totals(norm_grad, frames, per_group)
    second_sum = group_totals(norm_grad * normed, frames, per_group)
    first_sum, second_sum = lax.psum((first_sum, second_sum), "tile")
    first_chan = jnp.repeat(first_sum / group_size, per_group, axis=1)[:, None, None, :]
    second_chan = jnp.repeat(second_sum / group_size, per_group, axis=1)[:, None, None, :]
    d_acts = (inv_chan * (norm_grad - first_chan - normed * second_chan)).astype(jnp.bfloat16)
    flat_grads = cotangent.reshape(num_cells, -1)
    term_list = []
    for tap_t, tap_h, tap_w in tap_list:
        window_h = upsampled[
            tap_t : tap_t + frames, tap_h : tap_h + up_rows, tap_w : tap_w + up_cols
        ].reshape(num_cells, channels)
        term_list.append(
            lax.dot_general(
                window_h, flat_grads, (((0,), (0,)), ((), ())), preferred_element_type=jnp.float32
            )
        )
    whole_terms = jnp.stack(term_list, 1)
    whole_terms = lax.psum(whole_terms, "block")
    d_weights = lax.psum_scatter(whole_terms, "tile", scatter_dimension=0, tiled=True)
    return (d_acts, d_weights)


def solution(mesh):
    placed = (
        P("block", "tile", None, None),
        P(),
        P(),
        P("tile", None, None),
        P("block", "tile", None, None),
    )
    return jax.shard_map(
        shards,
        mesh=mesh,
        in_specs=placed,
        out_specs=(P("block", "tile", None, None), P("tile", None, None)),
        check_vma=False,
    )
```

profile of v0, /device:TPU:2, one launch (start us, length us, event | category | flops | bytes accessed | tf_op | source)
XLA Modules:
  0.0 430.7 jit_solution(1480891718286037013)
XLA Ops:
  11.7 56.1 %all-reduce.3 = (f32[2,32]{1,0:T(2,128)S(1)}, f32[2,32]{1,0:T(2,128)S(1)}) all-reduce(f32[2,32]{1,0:T(2,128)S(1)} %reduce_sum.86, f32[2,32]{1,0:T(2,128)S(1)} %reduce_sum.84), channel_id=1, replica_groups=mesh['block'=8,'tile'=32] {'tile'}, use_global_device_ids=true, to_apply=%region_5.0 | all-reduce | flops 128 | bytes 1024 | tf_op jit(solution)/shard_map/psum | solution.py:41
  68.8 1.9 collective-permute-start.1
  70.8 5.8 %collective-permute-start.2 = (bf16[4,1,128,192]{2,3,1,0:T(8,128)(2,1)S(1)}, bf16[4,1,128,192]{2,3,1,0:T(8,128)(2,1)S(1)}, u32[]{:S(2)}, u32[]{:S(2)}) collective-permute-start(bf16[4,1,128,192]{2,3,1,0:T(8,128)(2,1)S(1)} %get-tuple-element.44), channel_id=1, source_target_pairs={{1,0},{2,1},{3,2},{4,3},{5,4},{6,5},{7,6},{8,7},{9,8},{10,9},{11,1... | collective-permute-start | bytes 589832 | tf_op jit(solution)/shard_map/ppermute | solution.py:24
  83.8 2.5 fusion.110
  88.0 1.8 copy.86
  90.8 1.8 copy.85
  94.3 1.8 copy.83
  97.7 1.8 copy.82
  111.7 1.8 copy.76
  115.2 1.8 copy.74
  139.5 9.7 %concatenate.111 = bf16[2,1,2,64,2,5184]{5,3,4,2,0,1:T(8,128)(2,1)} concatenate(bf16[2,1,2,64,2,192]{5,3,4,2,0,1:T(8,128)(2,1)} %copy.92, bf16[2,1,2,64,2,192]{5,3,4,2,0,1:T(8,128)(2,1)S(1)} %copy.93, bf16[2,1,2,64,2,192]{5,3,4,2,0,1:T(8,128)(2,1)} %copy.94, bf16[2,1,2,64,2,192]{5,3,4,2,0,1:T(8,128)(2,1)} %copy.95, bf16[2,1,2,64,2,192]{5,3,4,2,0,1:T(8,128)(2,1)S(1)} %copy.96, ...), dimensions={5} | concatenate | bytes 10616832 | tf_op jit(solution)/shard_map/concatenate | solution.py:71
  149.2 8.6 %copy.119 = bf16[384,27,192]{0,2,1:T(8,128)(2,1)} copy(bf16[384,27,192]{2,1,0:T(8,128)(2,1)} %all-gather.2.cloned.1.call-done) | data formatting | bytes 7962624 | tf_op jit(solution)/shard_map/all_gather | solution.py:72
  157.8 6.7 %fusion.8 = f32[2,64,384]{2,1,0:T(8,128)S(1)} fusion(bf16[384,5184,1,1,1]{0,1,4,3,2:T(8,128)(2,1)} %bitcast.286, bf16[2,1,2,64,2,5184]{5,3,4,2,0,1:T(8,128)(2,1)} %concatenate.111), kind=kOutput, calls=%fused_computation.10 | convolution fusion | flops 2038579200 | bytes 9486336 | tf_op jit(solution)/shard_map/dot_general | solution.py:74
  164.7 4.4 %collective-permute-start.3 = (bf16[2,1,64,384]{3,2,1,0:T(8,128)(2,1)S(1)}, bf16[2,1,64,384]{3,2,1,0:T(8,128)(2,1)S(1)}, u32[]{:S(2)}, u32[]{:S(2)}) collective-permute-start(bf16[2,1,64,384]{3,2,1,0:T(8,128)(2,1)S(1)} %get-tuple-element.45), channel_id=1, source_target_pairs={{0,32},{32,64},{64,96},{96,128},{128,160},{160,192},{192,224},{1,3... | collective-permute-start | bytes 294920 | tf_op jit(solution)/shard_map/ppermute | solution.py:13
  169.1 2.2 collective-permute-done.3
  171.3 5.1 %collective-permute-start.5 = (bf16[4,1,64,384]{3,2,1,0:T(8,128)(2,1)S(1)}, bf16[4,1,64,384]{3,2,1,0:T(8,128)(2,1)S(1)}, u32[]{:S(2)}, u32[]{:S(2)}) collective-permute-start(bf16[4,1,64,384]{3,2,1,0:T(8,128)(2,1)S(1)} %pad_maximum_fusion.3), channel_id=1, source_target_pairs={{1,0},{2,1},{3,2},{4,3},{5,4},{6,5},{7,6},{8,7},{9,8},{10,9},{11,1... | collective-permute-start | bytes 589832 | tf_op jit(solution)/shard_map/ppermute | solution.py:24
  176.4 2.1 collective-permute-start.4
  179.5 5.9 %collective-permute-done.4 = bf16[4,1,64,384]{3,2,1,0:T(8,128)(2,1)S(1)} collective-permute-done((bf16[4,1,64,384]{3,2,1,0:T(8,128)(2,1)S(1)}, bf16[4,1,64,384]{3,2,1,0:T(8,128)(2,1)S(1)}, u32[]{:S(2)}, u32[]{:S(2)}) %collective-permute-start.4) | collective-permute-done | bytes 196640 | tf_op jit(solution)/shard_map/ppermute | solution.py:23
  185.7 3.2 broadcast_in_dim.26
  188.9 5.1 %reshape.166 = bf16[4,6,128,384]{3,2,1,0:T(8,128)(2,1)S(1)} reshape(bf16[4,6,64,2,384]{4,3,2,1,0:T(2,128)(2,1)} %broadcast_in_dim.26) | data formatting | bytes 4718592 | tf_op jit(solution)/shard_map/reshape | solution.py:53
  220.9 12.0 %copy.120 = f32[384,27,192]{2,1,0:T(8,128)} copy(f32[384,27,192]{0,2,1:T(8,128)} %fusion.11) | data formatting | bytes 15925248 | tf_op jit(solution)/shard_map/stack | solution.py:98
  233.4 53.0 %all-reduce.2 = (f32[2,32]{1,0:T(2,128)S(1)}, f32[2,32]{1,0:T(2,128)S(1)}) all-reduce(f32[2,32]{1,0:T(2,128)S(1)} %reduce_sum.92, f32[2,32]{1,0:T(2,128)S(1)} %reduce_sum.90), channel_id=1, replica_groups=mesh['block'=8,'tile'=32] {'tile'}, use_global_device_ids=true, to_apply=%region_12.13 | all-reduce | flops 128 | bytes 1024 | tf_op jit(solution)/shard_map/psum | solution.py:83
  286.4 60.6 %reduce-scatter.2.cloned.1.call-done = f32[12,27,192]{2,1,0:T(8,128)} async-done(((f32[384,27,192]{2,1,0:T(8,128)}), f32[12,27,192]{2,1,0:T(8,128)}) %reduce-scatter.2.cloned.1.call-update) | async-done | bytes 248848 | tf_op jit(solution)/shard_map/reduce_scatter | solution.py:100
  348.1 74.3 %all-reduce.6.cloned.1.call-done = f32[12,27,192]{2,1,0:T(8,128)} async-done(((f32[12,27,192]{2,1,0:T(8,128)}), f32[12,27,192]{2,1,0:T(8,128)}) %all-reduce.6.cloned.1.call-update) | async-done | bytes 248848 | tf_op jit(solution)/shard_map/psum | solution.py:99
  (126 shorter events, 86.6 us)
Async XLA Ops:
  7.2 142.0 %all-gather.2.cloned.1.call-start = ((), (), s32[]{:S(2)}) async-start(), calls=%async_computation.1 | async-start | bytes 6488064 | tf_op jit(solution)/shard_map/all_gather | solution.py:72
  7.9 339.1 %reduce-scatter.2.cloned.1.call-start = ((), (), s32[]{:S(2)}) async-start(), calls=%async_computation.2 | async-start | bytes 12976128 | tf_op jit(solution)/shard_map/reduce_scatter | solution.py:100
  7.9 60.8 %collective-permute-start = (bf16[2,2,128,192]{2,3,1,0:T(8,128)(2,1)}, bf16[2,2,128,192]{2,3,1,0:T(8,128)(2,1)S(1)}, u32[]{:S(2)}, u32[]{:S(2)}) collective-permute-start(bf16[2,2,128,192]{2,3,1,0:T(8,128)(2,1)} %param.9), channel_id=1, source_target_pairs={{32,0},{64,32},{96,64},{128,96},{160,128},{192,160},{224,192},{33,... | collective-permute-start | bytes 589832 | tf_op jit(solution)/shard_map/ppermute | solution.py:13
  68.8 9.1 %collective-permute-start.1 = (bf16[4,1,128,192]{2,3,1,0:T(8,128)(2,1)S(1)}, bf16[4,1,128,192]{2,3,1,0:T(8,128)(2,1)S(1)}, u32[]{:S(2)}, u32[]{:S(2)}) collective-permute-start(bf16[4,1,128,192]{2,3,1,0:T(8,128)(2,1)S(1)} %get-tuple-element.43), channel_id=1, source_target_pairs={{0,1},{1,2},{2,3},{3,4},{4,5},{5,6},{6,7},{7,8},{8,9},{9,10},{10,1... | collective-permute-start | bytes 589832 | tf_op jit(solution)/shard_map/ppermute | solution.py:23
  70.8 8.9 %collective-permute-start.2 = (bf16[4,1,128,192]{2,3,1,0:T(8,128)(2,1)S(1)}, bf16[4,1,128,192]{2,3,1,0:T(8,128)(2,1)S(1)}, u32[]{:S(2)}, u32[]{:S(2)}) collective-permute-start(bf16[4,1,128,192]{2,3,1,0:T(8,128)(2,1)S(1)} %get-tuple-element.44), channel_id=1, source_target_pairs={{1,0},{2,1},{3,2},{4,3},{5,4},{6,5},{7,6},{8,7},{9,8},{10,9},{11,1... | collective-permute-start | bytes 589832 | tf_op jit(solution)/shard_map/ppermute | solution.py:24
  157.7 6.7 %copy-start.1 = (bf16[2,1,64,384]{3,2,1,0:T(8,128)(2,1)S(1)}, bf16[2,1,64,384]{3,2,1,0:T(8,128)(2,1)}, u32[]{:S(2)}) copy-start(bf16[2,1,64,384]{3,2,1,0:T(8,128)(2,1)} %param.5) | copy-start | bytes 294916
  157.7 6.7 %copy-start.2 = (f32[384]{0:T(512)S(1)}, f32[384]{0:T(512)}, u32[]{:S(2)}) copy-start(f32[384]{0:T(512)} %param.7) | copy-start | bytes 4612
  157.8 6.7 %copy-start.3 = (f32[384]{0:T(512)S(1)}, f32[384]{0:T(512)}, u32[]{:S(2)}) copy-start(f32[384]{0:T(512)} %param.6) | copy-start | bytes 4612
  164.7 6.6 %collective-permute-start.3 = (bf16[2,1,64,384]{3,2,1,0:T(8,128)(2,1)S(1)}, bf16[2,1,64,384]{3,2,1,0:T(8,128)(2,1)S(1)}, u32[]{:S(2)}, u32[]{:S(2)}) collective-permute-start(bf16[2,1,64,384]{3,2,1,0:T(8,128)(2,1)S(1)} %get-tuple-element.45), channel_id=1, source_target_pairs={{0,32},{32,64},{64,96},{96,128},{128,160},{160,192},{192,224},{1,3... | collective-permute-start | bytes 294920 | tf_op jit(solution)/shard_map/ppermute | solution.py:13
  171.3 8.2 %collective-permute-start.5 = (bf16[4,1,64,384]{3,2,1,0:T(8,128)(2,1)S(1)}, bf16[4,1,64,384]{3,2,1,0:T(8,128)(2,1)S(1)}, u32[]{:S(2)}, u32[]{:S(2)}) collective-permute-start(bf16[4,1,64,384]{3,2,1,0:T(8,128)(2,1)S(1)} %pad_maximum_fusion.3), channel_id=1, source_target_pairs={{1,0},{2,1},{3,2},{4,3},{5,4},{6,5},{7,6},{8,7},{9,8},{10,9},{11,1... | collective-permute-start | bytes 589832 | tf_op jit(solution)/shard_map/ppermute | solution.py:24
  176.4 9.1 %collective-permute-start.4 = (bf16[4,1,64,384]{3,2,1,0:T(8,128)(2,1)S(1)}, bf16[4,1,64,384]{3,2,1,0:T(8,128)(2,1)S(1)}, u32[]{:S(2)}, u32[]{:S(2)}) collective-permute-start(bf16[4,1,64,384]{3,2,1,0:T(8,128)(2,1)S(1)} %pad_maximum_fusion.3), channel_id=1, source_target_pairs={{0,1},{1,2},{2,3},{3,4},{4,5},{5,6},{6,7},{7,8},{8,9},{9,10},{10,1... | collective-permute-start | bytes 589832 | tf_op jit(solution)/shard_map/ppermute | solution.py:23
  188.9 5.3 %copy-start = (bf16[2,2,128,192]{2,3,1,0:T(8,128)(2,1)S(1)}, bf16[2,2,128,192]{2,3,1,0:T(8,128)(2,1)}, u32[]{:S(2)}) copy-start(bf16[2,2,128,192]{2,3,1,0:T(8,128)(2,1)} %param.9) | copy-start | bytes 589828
  232.9 189.4 %all-reduce.6.cloned.1.call-start = ((), (), s32[]{:S(2)}) async-start(), calls=%async_computation.3 | async-start | bytes 786432 | tf_op jit(solution)/shard_map/psum | solution.py:99
Sparse Core Ops, SparseCore 0:
  10.5 56.0 all-gather.1
  233.1 113.8 reduce-scatter.1
  349.3 72.9 all-reduce.5
where the time goes:
time: 433 us; the launch traced here: 431 us
  waiting for transfers between devices  147 us (34%)
  blocking collectives  109 us (25%)
  local copies, waits for them, and re-layouts  102 us (24%)
  matrix products  33.4 us (8%)
  starting transfers between devices  20.7 us (5%)
  between operations  14.2 us (3%)
    psum x1, waiting for transfers between devices, shards(): whole_terms = lax.psum(whole_terms, 'block')  74.3 us
    reduce_scatter x1, waiting for transfers between devices, shards(): lax.psum_scatter(whole_terms, 'tile', scatter_dimension=0, tiled=True)  60.6 us
    psum x1, blocking collectives, shards(): stat_sum, stat_sq = lax.psum((stat_sum, stat_sq), 'tile')  56.1 us
    psum x1, blocking collectives, shards(): first_sum, second_sum = lax.psum((first_sum, second_sum), 'tile')  53 us
    concatenate x28, local copies, waits for them, and re-layouts, shards(): columns = jnp.concatenate(windows, 1)  34.5 us
    slice x26, local copies, waits for them, and re-layouts, shards(): grad_field[2 - tap_t:2 - tap_t + frames, 2 - tap_h:2 - tap_h + up_rows, 2...  33.3 us
    dot_general x27, matrix products, shards(): lax.dot_general(window_h, flat_grads, (((0,), (0,)), ((), ())), preferred...  26.7 us
    another operation x1, local copies, waits for them, and re-layouts, shards(): whole_terms = jnp.stack(term_list, 1)  12 us
  transfers between devices with their start and end apart: 9, of which 7 were waited for; matrix products, arithmetic and copies ran while one was open for 17% of the time, Pallas kernels for 0%

commit v1 on v0

--- a/solution.py
+++ b/solution.py
@@ -96,7 +96,7 @@
             )
         )
     whole_terms = jnp.stack(term_list, 1)
-    whole_terms = lax.psum(whole_terms, "block")
+    whole_terms = jnp.sum(lax.all_gather(whole_terms, axis_name="block"), axis=0)
     d_weights = lax.psum_scatter(whole_terms, "tile", scatter_dimension=0, tiled=True)
     return (d_acts, d_weights)
 

time: 433 us -> 1050 us (2.42)
  waiting for transfers between devices: 147 us -> 681 us
  local copies, waits for them, and re-layouts: 102 us -> 143 us
  other arithmetic: 3.85 us -> 39.7 us
    all_gather x0 -> x1, waiting for transfers between devices: none -> 615 us  [shards(): lax.all_gather(whole_terms, axis_name='block')]
    psum x1 -> x0, waiting for transfers between devices: 74.3 us -> none  [shards(): whole_terms = lax.psum(whole_terms, 'block')]
    unnamed x11, local copies, waits for them, and re-layouts: 3.83 us -> 45.2 us
    reduce_sum x0 -> x1, other arithmetic: none -> 35.9 us  [shards(): jnp.sum(lax.all_gather(whole_terms, axis_name='block'), axis=0)]
    another operation x1 -> x0, local copies, waits for them, and re-layouts: 12 us -> none  [shards(): whole_terms = jnp.stack(term_list, 1)]
    reduce_sum x0 -> x1, local copies, waits for them, and re-layouts: none -> 12 us  [shards(): jnp.sum(lax.all_gather(whole_terms, axis_name='block'), axis=0)]
  transfers between devices with their start and end apart: 9 -> 9, of which waited for: 7 -> 7; matrix products, arithmetic and copies ran while one was open for 17% -> 7% of each run, Pallas kernels for 0% -> 0%
where the time goes in v1:
time: 1050 us; the launch traced here: 1040 us
  waiting for transfers between devices  681 us (65%)
  local copies, waits for them, and re-layouts  143 us (14%)
  blocking collectives  111 us (11%)
  other arithmetic  39.7 us (4%)
  matrix products  33.5 us (3%)
  starting transfers between devices  20.9 us (2%)
  between operations  14.2 us (1%)
    all_gather x1, waiting for transfers between devices, shards(): lax.all_gather(whole_terms, axis_name='block')  615 us
    psum x1, blocking collectives, shards(): stat_sum, stat_sq = lax.psum((stat_sum, stat_sq), 'tile')  56.1 us
    psum x1, blocking collectives, shards(): first_sum, second_sum = lax.psum((first_sum, second_sum), 'tile')  55 us
    reduce_scatter x1, waiting for transfers between devices, shards(): lax.psum_scatter(whole_terms, 'tile', scatter_dimension=0, tiled=True)  53.7 us
    unnamed x11, local copies, waits for them, and re-layouts  45.2 us
    reduce_sum x1, other arithmetic, shards(): jnp.sum(lax.all_gather(whole_terms, axis_name='block'), axis=0)  35.9 us
    concatenate x28, local copies, waits for them, and re-layouts, shards(): columns = jnp.concatenate(windows, 1)  34.5 us
    slice x26, local copies, waits for them, and re-layouts, shards(): grad_field[2 - tap_t:2 - tap_t + frames, 2 - tap_h:2 - tap_h + up_rows, 2...  33.3 us
  transfers between devices with their start and end apart: 9, of which 7 were waited for; matrix products, arithmetic and copies ran while one was open for 7% of the time, Pallas kernels for 0%

profile of v1, /device:TPU:2, one launch (start us, length us, event | category | flops | bytes accessed | tf_op | source)
XLA Modules:
  0.0 1043.9 jit_solution(15683295171595610901)
XLA Ops:
  11.7 56.1 %all-reduce.3 = (f32[2,32]{1,0:T(2,128)S(1)}, f32[2,32]{1,0:T(2,128)S(1)}) all-reduce(f32[2,32]{1,0:T(2,128)S(1)} %reduce_sum.95, f32[2,32]{1,0:T(2,128)S(1)} %reduce_sum.93), channel_id=1, replica_groups=mesh['block'=8,'tile'=32] {'tile'}, use_global_device_ids=true, to_apply=%region_5.0 | all-reduce | flops 128 | bytes 1024 | tf_op jit(solution)/shard_map/psum | solution.py:41
  68.8 1.9 collective-permute-start.1
  70.8 5.8 collective-permute-start.2
  83.8 2.5 fusion.110
  88.0 1.8 copy.140
  90.8 1.8 copy.139
  111.7 1.8 copy.130
  115.2 1.8 copy.128
  139.5 9.7 concatenate.111
  149.2 8.6 copy.173
  157.8 6.7 fusion.8
  164.7 4.4 collective-permute-start.3
  169.1 2.2 collective-permute-done.3
  171.3 5.1 collective-permute-start.5
  176.4 2.1 collective-permute-start.4
  179.5 5.9 collective-permute-done.4
  185.7 3.2 broadcast_in_dim.26
  188.9 5.1 reshape.166
  221.3 615.0 %all-gather.6.cloned.1.call-done = f32[3072,27,192]{0,2,1:T(8,128)} async-done(((f32[384,27,192]{0,2,1:T(8,128)}), f32[3072,27,192]{0,2,1:T(8,128)}) %all-gather.6.cloned.1.call-update) | async-done | bytes 63701008 | tf_op jit(solution)/shard_map/all_gather | solution.py:99
  836.3 43.1 %copy.203 = f32[648,8,8,384]{3,2,1,0:T(8,128)} copy(f32[648,8,8,384]{3,1,2,0:T(8,128)} %bitcast.292) | data formatting | bytes 127401984
  879.4 35.9 %reduce_sum.102 = f32[384,27,192]{0,2,1:T(8,128)} reduce(f32[8,384,27,192]{1,0,3,2:T(8,128)} %bitcast.291, f32[]{:T(128)} %constant.10.clone.1), dimensions={0}, to_apply=%region_13.14 | reduce | flops 13934592 | bytes 71663616 | tf_op jit(solution)/shard_map/reduce_sum | solution.py:99
  915.2 12.0 %copy.174 = f32[384,27,192]{2,1,0:T(8,128)} copy(f32[384,27,192]{0,2,1:T(8,128)} %reduce_sum.102) | data formatting | bytes 15925248 | tf_op jit(solution)/shard_map/reduce_sum | solution.py:99
  927.6 55.0 %all-reduce.2 = (f32[2,32]{1,0:T(2,128)S(1)}, f32[2,32]{1,0:T(2,128)S(1)}) all-reduce(f32[2,32]{1,0:T(2,128)S(1)} %reduce_sum.101, f32[2,32]{1,0:T(2,128)S(1)} %reduce_sum.99), channel_id=1, replica_groups=mesh['block'=8,'tile'=32] {'tile'}, use_global_device_ids=true, to_apply=%region_12.13 | all-reduce | flops 128 | bytes 1024 | tf_op jit(solution)/shard_map/psum | solution.py:83
  983.7 53.7 %reduce-scatter.2.cloned.1.call-done = f32[12,27,192]{2,1,0:T(8,128)} async-done(((f32[384,27,192]{2,1,0:T(8,128)}), f32[12,27,192]{2,1,0:T(8,128)}) %reduce-scatter.2.cloned.1.call-update) | async-done | bytes 248848 | tf_op jit(solution)/shard_map/reduce_scatter | solution.py:100
  (127 shorter events, 88.7 us)
Async XLA Ops:
  7.2 142.0 %all-gather.4.cloned.1.call-start = ((), (), s32[]{:S(2)}) async-start(), calls=%async_computation.1 | async-start | bytes 6488064 | tf_op jit(solution)/shard_map/all_gather | solution.py:72
  7.9 828.4 %all-gather.6.cloned.1.call-start = ((), (), s32[]{:S(2)}) async-start(), calls=%async_computation.3 | async-start | bytes 71663616 | tf_op jit(solution)/shard_map/all_gather | solution.py:99
  7.9 60.8 %collective-permute-start = (bf16[2,2,128,192]{2,3,1,0:T(8,128)(2,1)}, bf16[2,2,128,192]{2,3,1,0:T(8,128)(2,1)S(1)}, u32[]{:S(2)}, u32[]{:S(2)}) collective-permute-start(bf16[2,2,128,192]{2,3,1,0:T(8,128)(2,1)} %param.9), channel_id=1, source_target_pairs={{32,0},{64,32},{96,64},{128,96},{160,128},{192,160},{224,192},{33,... | collective-permute-start | bytes 589832 | tf_op jit(solution)/shard_map/ppermute | solution.py:13
  68.8 9.1 collective-permute-start.1
  70.8 8.9 collective-permute-start.2
  157.7 6.7 copy-start.1
  157.7 6.7 copy-start.2
  157.8 6.7 copy-start.3
  164.7 6.6 collective-permute-start.3
  171.3 8.2 collective-permute-start.5
  176.4 9.1 collective-permute-start.4
  188.9 5.3 copy-start
  221.0 816.4 %reduce-scatter.2.cloned.1.call-start = ((), (), s32[]{:S(2)}) async-start(), calls=%async_computation.2 | async-start | bytes 12976128 | tf_op jit(solution)/shard_map/reduce_scatter | solution.py:100
Sparse Core Ops, SparseCore 0:
  10.5 56.0 all-gather.3
  221.1 615.1 all-gather.5
  927.3 110.0 reduce-scatter.1
